TPU v7x, 32 devices: a whole 2x2x4 slice. The times are simulated.
32 devices in a mesh: chan: 8 (over y, x, core), win: 4 (over z).
Axes of the slice: x: 2, y: 2, z: 4, core: 2. Of those that a mesh axis runs over, the one named last changes fastest.
Arguments:
- records: float32 [16, 1024, 256], P('win', 'chan'), may hold values from -180 to 180
- sources: int32 [32], replicated, may hold values from 0 to 255, as said below
Outputs:
- correlations: float32 [32, 256, 256], P('win', None, 'chan')
Inputs may be any that keep to these rules, and one draw needn't show every extreme that they name: `sources`: source s is one of the channels s * 8 to (s + 1) * 8 - 1; the first source is channel 0 and the last is channel 256 - 1.
All inputs are finite; a program needn't handle non-finite values.
Results may differ from a plain program's by a relative error of at most 0.00022.
Values sent between devices are 32-bit elements; how exact they have to be, the bound alone decides.
A program may use at most 64 MiB of HBM per device.

v0:
```python
import math
import jax
import jax.numpy as jnp
from jax import lax
from jax.sharding import PartitionSpec as P

HIGHEST = lax.Precision.HIGHEST
AMPLITUDE_FLOOR = 0.25
WHITE_EPSILON = 1e-06


def fourier_table(length):
    freq_count = length // 2
    freqs = jnp.arange(freq_count, dtype=jnp.int32)[:, None]
    sample_index = jnp.arange(length, dtype=jnp.int32)[None, :]
    angles = (freqs * sample_index % length).astype(jnp.float32) * (2.0 * math.pi / length)
    return jnp.concatenate([jnp.cos(angles), -jnp.sin(angles)], axis=0)


def band_table(freq_count, reach):
    rows_index = jnp.arange(freq_count, dtype=jnp.int32)[:, None]
    cols_index = jnp.arange(freq_count, dtype=jnp.int32)[None, :]
    return (jnp.abs(rows_index - cols_index) <= reach).astype(jnp.float32)


def inverse_table(length, lag_count, first_bin, bin_count, factor):
    freqs = first_bin + jnp.arange(bin_count, dtype=jnp.int32)
    lag_index = jnp.arange(lag_count, dtype=jnp.int32) - lag_count // 2
    angles = (lag_index[:, None] * freqs[None, :] % length).astype(jnp.float32) * (
        2.0 * math.pi / length
    )
    weights = jnp.where(freqs == 0, 1.0, 2.0).astype(jnp.float32)[None, :] * factor
    return jnp.concatenate([weights * jnp.cos(angles), -weights * jnp.sin(angles)], axis=1)


def running_level(padded, time_count, window_span):
    window_total = padded.shape[0]
    chans = padded.shape[2]
    running = jnp.concatenate(
        [jnp.zeros((window_total, 1, chans), jnp.float32), jnp.cumsum(jnp.abs(padded), axis=1)],
        axis=1,
    )
    return (running[:, window_span:] - running[:, :time_count]) / window_span


def local(records, sources):
    chan_count = lax.axis_size("chan")
    local_windows, local_time, all_channels = records.shape
    length = local_time * chan_count
    freq_count = length // 2
    chan_width = all_channels // chan_count
    half_width = min(16, local_time)
    smooth_reach = length // 32
    window_span = 2 * half_width + 1
    lag_count = length // 4
    forward = fourier_table(length)
    band_matrix = band_table(freq_count, smooth_reach)
    pieces = lax.all_to_all(records, "chan", split_axis=2, concat_axis=1, tiled=True)
    padded = jnp.pad(pieces, ((0, 0), (half_width, half_width), (0, 0)))
    amplitude = running_level(padded, length, window_span)
    whiten_pieces = pieces / jnp.maximum(amplitude, AMPLITUDE_FLOOR)
    spectrum = jnp.einsum("kt,wtc->wkc", forward, whiten_pieces, precision=HIGHEST)
    real_part = spectrum[:, :freq_count]
    imag_part = spectrum[:, freq_count:]
    magnitude = jnp.sqrt(real_part * real_part + imag_part * imag_part)
    smoothed = (
        jnp.einsum("jk,wkc->wjc", band_matrix, magnitude, precision=HIGHEST)
        / (2 * smooth_reach + 1)
        + WHITE_EPSILON
    )
    whitened = jnp.stack([real_part / smoothed, imag_part / smoothed], axis=1)
    band_data = lax.all_to_all(whitened, "win", split_axis=2, concat_axis=0, tiled=True)
    total_windows = band_data.shape[0]
    band_count = band_data.shape[2]
    source_count = sources.shape[0]
    chan_index = lax.axis_index("chan")
    channel_ids = jnp.arange(chan_width, dtype=jnp.int32)
    per_device = source_count // chan_count
    owned_local = (
        lax.dynamic_slice_in_dim(sources, chan_index * per_device, per_device)
        - chan_index * chan_width
    )
    selector = (owned_local[:, None] == channel_ids[None, :]).astype(jnp.float32)
    chosen = jnp.einsum("sc,wafc->wafs", selector, band_data, precision=HIGHEST)
    spectra = lax.all_gather(chosen, "chan", axis=3, tiled=True)
    source_real = spectra[:, 0]
    source_imag = spectra[:, 1]
    white_real = band_data[:, 0]
    white_imag = band_data[:, 1]
    cross_real = jnp.einsum(
        "wfs,wfc->fsc", source_real, white_real, precision=HIGHEST
    ) + jnp.einsum("wfs,wfc->fsc", source_imag, white_imag, precision=HIGHEST)
    cross_imag = jnp.einsum(
        "wfs,wfc->fsc", source_real, white_imag, precision=HIGHEST
    ) - jnp.einsum("wfs,wfc->fsc", source_imag, white_real, precision=HIGHEST)
    stacked = jnp.stack([cross_real, cross_imag])
    factor = 1.0 / math.sqrt(total_windows * freq_count)
    band_start = lax.axis_index("win") * band_count
    band_table_part = inverse_table(length, lag_count, band_start, band_count, factor).reshape(
        lag_count, 2, band_count
    )
    return lax.psum_scatter(
        jnp.einsum("tak,aksc->stc", band_table_part, stacked, precision=HIGHEST),
        "win",
        scatter_dimension=0,
        tiled=True,
    )


def solution(mesh):
    placed = (P("win", "chan", None), P())
    return jax.shard_map(
        local, mesh=mesh, in_specs=placed, out_specs=P("win", None, "chan"), check_vma=False
    )
```

profile of v0, /device:TPU:0, one launch (start us, length us, event | category | flops | bytes accessed | tf_op | source)
XLA Modules:
  0.0 168.4 jit_solution(1420910097086612107)
XLA Ops:
  6.5 2.1 %copy.58 = f32[4,128,256]{1,0,2:T(4,128)} copy(f32[4,128,256]{2,1,0:T(8,128)} %param.2) | data formatting | bytes 1048576 | tf_op args[0]
  8.6 5.2 %all-to-all-start = ((f32[4,128,256]{1,0,2:T(4,128)}), f32[4,128,256]{1,0,2:T(4,128)S(1)}, u32[]{:S(2)}, u32[]{:S(2)}) async-start(f32[4,128,256]{1,0,2:T(4,128)} %copy.58), calls=%async_computation | async-start | bytes 1048576 | tf_op jit(solution)/shard_map/all_to_all | solution.py:58
  13.8 9.2 %sine_negate_fusion = (f32[512,1024]{1,0:T(8,128)}, f32[512,1024]{1,0:T(8,128)}) fusion(), kind=kLoop, calls=%fused_computation.15 | loop fusion | flops 7864320 | bytes 4194304 | tf_op jit(solution)/shard_map/neg | solution.py:17
  23.0 0.5 all-to-all-done
  23.6 0.2 abs_bitcast_fusion
  23.9 0.1 reshape.194
  24.0 36.3 %reduce-window.6 = f32[4,32,9,128]{3,2,1,0:T(8,128)S(1)} reduce-window(f32[4,32,9,128]{3,2,1,0:T(8,128)S(1)} %reshape.194, f32[]{:T(128)} %constant.22.clone.1), window={size=1x1x1x128 pad=0_0x0_0x0_0x127_0}, to_apply=%region_0.1 | reduce-window | flops 18726912 | bytes 1179652 | tf_op jit(solution)/shard_map/reduce-window
  60.3 0.3 slice.45
  60.6 0.4 copy.61
  61.0 0.1 copy.62
  61.1 0.3 broadcast_add_fusion
  61.4 0.1 reduce_window_sum.16
  61.5 6.6 %fusion.14 = f32[4,1024,32]{1,2,0:T(8,128)S(1)} fusion(f32[512,1024]{1,0:T(8,128)} %get-tuple-element.13, f32[512,1024]{1,0:T(8,128)} %get-tuple-element.14, f32[4,1056,32]{1,2,0:T(8,128)S(1)} %bitcast.87, f32[4,1152,32]{1,2,0:T(8,128)S(1)} %bitcast.86, f32[4,8,4,8,128]{4,3,2,1,0:T(8,128)S(1)} %bitcast.84), kind=kOutput, calls=%fused_computation.20 | convolution fusion | flops 1612185600 | bytes 6356992 | tf_op jit(solution)/shard_map/kt,wtc->wkc/dot_general | solution.py:62
  68.1 0.7 divide_bitcast_fusion.1
  68.9 1.1 copy.63
  69.9 0.0 copy-start.2
  70.0 2.1 %reshape.201 = f32[4,1,32768]{2,1,0:T(1,128)} reshape(f32[512,2,4,32]{3,2,1,0:T(4,128)S(1)} %bitcast.79) | data formatting | bytes 1048576
  72.0 4.9 %all-to-all-start.1 = ((f32[4,1,32768]{2,1,0:T(1,128)}), f32[4,1,32768]{2,1,0:T(1,128)S(1)}, u32[]{:S(2)}, u32[]{:S(2)}) async-start(f32[4,1,32768]{2,1,0:T(1,128)} %reshape.201), calls=%async_computation.1 | async-start | bytes 1048576 | tf_op jit(solution)/shard_map/all_to_all | solution.py:72
  76.9 0.0 reduce-scatter.2.cloned.1.call-start
  76.9 0.0 copy-done.2
  76.9 0.1 dynamic-slice_subtract_fusion
  77.0 1.3 cosine_multiply_fusion
  78.2 13.3 %all-to-all-done.1 = f32[4,1,32768]{2,1,0:T(1,128)S(1)} async-done(((f32[4,1,32768]{2,1,0:T(1,128)}), f32[4,1,32768]{2,1,0:T(1,128)S(1)}, u32[]{:S(2)}, u32[]{:S(2)}) %all-to-all-start.1) | async-done | bytes 524320 | tf_op jit(solution)/shard_map/all_to_all | solution.py:72
  91.5 0.5 broadcast.245
  92.0 2.1 %reduce = f32[4,32768]{1,0:T(4,128)S(1)} reduce(f32[4,1,32768]{2,1,0:T(1,128)S(1)} %all-to-all-done.1, f32[]{:T(128)} %broadcast.245), dimensions={1}, to_apply=%all_to_all.30.reduce_sub_computation | reduce | bytes 1048580 | tf_op jit(solution)/shard_map/all_to_all | solution.py:72
  94.2 1.1 reshape.202
  95.3 0.8 copy.64
  96.2 0.3 fusion.49
  96.5 10.0 %all_gather.3 = f32[16,2,128,32]{2,0,1,3:T(8,128)S(1)} all-gather(f32[16,2,128,4]{2,0,1,3:T(8,128)S(1)} %copy.65), channel_id=1, replica_groups=mesh['chan'=8,'win'=4] {'chan'}, dimensions={3}, use_global_device_ids=true | all-gather | bytes 589824 | tf_op jit(solution)/shard_map/all_gather | solution.py:85
  106.5 0.7 fusion.60
  107.2 0.5 copy.77
  107.7 0.5 copy.67
  108.2 1.5 copy.78
  109.7 1.4 copy.69
  111.1 0.0 copy-start
  111.1 3.6 %fusion.21 = f32[128,32,32]{2,1,0:T(8,128)S(1)} fusion(f32[16,128,32]{2,0,1:T(8,128)S(1)} %copy.67, f32[16,1,128,32]{3,0,2,1:T(8,128)S(1)} %copy.77), kind=kOutput, calls=%fused_computation.28 | convolution fusion | flops 25165824 | bytes 1048576 | tf_op jit(solution)/shard_map/wfs,wfc->fsc/dot_general | solution.py:90
  114.7 0.0 copy-done
  114.7 3.6 %fusion.19 = f32[128,32,32]{2,1,0:T(8,128)S(1)} fusion(f32[16,128,32]{2,0,1:T(8,128)S(1)} %copy-done, f32[16,1,128,32]{3,0,2,1:T(8,128)S(1)} %copy.77), kind=kOutput, calls=%fused_computation.26 | convolution fusion | flops 25165824 | bytes 1048576 | tf_op jit(solution)/shard_map/wfs,wfc->fsc/dot_general | solution.py:93
  118.4 3.9 %add_bitcast_fusion = f32[1,128,32,32]{3,2,1,0:T(8,128)S(1)} fusion(f32[128,32,32]{2,1,0:T(8,128)S(1)} %fusion.21, f32[16,128,32]{2,0,1:T(8,128)S(1)} %copy-done, f32[16,1,128,32]{3,0,2,1:T(8,128)S(1)} %copy.78), kind=kOutput, calls=%fused_computation.14 | convolution fusion | flops 25296896 | bytes 1572864 | tf_op jit(solution)/shard_map/wfs,wfc->fsc/dot_general | solution.py:92
  122.3 3.7 %subtract_bitcast_fusion = f32[1,128,32,32]{3,2,1,0:T(8,128)S(1)} fusion(f32[128,32,32]{2,1,0:T(8,128)S(1)} %fusion.19, f32[16,128,32]{2,0,1:T(8,128)S(1)} %copy.67, f32[16,1,128,32]{3,0,2,1:T(8,128)S(1)} %copy.78), kind=kOutput, calls=%fused_computation.13 | convolution fusion | flops 25296896 | bytes 1572864 | tf_op jit(solution)/shard_map/wfs,wfc->fsc/dot_general | solution.py:95
  126.0 0.0 copy-start.1
  126.0 0.6 pad_maximum_fusion
  126.6 0.3 copy-done.1
  126.9 9.1 %fusion.11 = f32[32,256,32]{1,2,0:T(8,128)} fusion(f32[2,128,32,32]{3,2,1,0:T(8,128)S(1)} %pad_maximum_fusion, f32[256,1,128]{2,0,1:T(8,128)S(1)} %copy-done.1, f32[256,1,128]{2,0,1:T(8,128)S(1)} %get-tuple-element.11), kind=kOutput, calls=%fused_computation.19 | convolution fusion | flops 805371904 | bytes 2359296 | tf_op jit(solution)/shard_map/tak,aksc->stc/dot_general | solution.py:103
  136.0 0.0 reduce-scatter.2.cloned.1.call-update
  136.0 25.6 %reduce-scatter.2.cloned.1.call-done = f32[8,256,32]{1,2,0:T(8,128)} async-done(((f32[32,256,32]{1,2,0:T(8,128)}), f32[8,256,32]{1,2,0:T(8,128)}) %reduce-scatter.2.cloned.1.call-update) | async-done | bytes 262160 | tf_op jit(solution)/shard_map/reduce_scatter | solution.py:102
  (11 shorter events, 0.2 us)
Async XLA Ops:
  8.6 14.9 %all-to-all-start = ((f32[4,128,256]{1,0,2:T(4,128)}), f32[4,128,256]{1,0,2:T(4,128)S(1)}, u32[]{:S(2)}, u32[]{:S(2)}) async-start(f32[4,128,256]{1,0,2:T(4,128)} %copy.58), calls=%async_computation | async-start | bytes 1048576 | tf_op jit(solution)/shard_map/all_to_all | solution.py:58
  69.9 6.9 %copy-start.2 = (s32[32]{0:T(128)S(1)}, s32[32]{0:T(128)}, u32[]{:S(2)}) copy-start(s32[32]{0:T(128)} %param.3) | copy-start | bytes 388
  72.0 19.5 %all-to-all-start.1 = ((f32[4,1,32768]{2,1,0:T(1,128)}), f32[4,1,32768]{2,1,0:T(1,128)S(1)}, u32[]{:S(2)}, u32[]{:S(2)}) async-start(f32[4,1,32768]{2,1,0:T(1,128)} %reshape.201), calls=%async_computation.1 | async-start | bytes 1048576 | tf_op jit(solution)/shard_map/all_to_all | solution.py:72
  76.9 84.7 %reduce-scatter.2.cloned.1.call-start = ((), (), s32[]{:S(2)}) async-start(), calls=%async_computation.3 | async-start | bytes 1310720 | tf_op jit(solution)/shard_map/reduce_scatter | solution.py:102
  111.1 3.6 %copy-start = (f32[16,128,32]{2,0,1:T(8,128)S(1)}, f32[16,128,32]{2,0,1:T(8,128)}, u32[]{:S(2)}) copy-start(f32[16,128,32]{2,0,1:T(8,128)} %copy.69) | copy-start | bytes 786436
  126.0 0.9 copy-start.1
Sparse Core Ops, SparseCore 0:
  136.1 25.3 reduce-scatter.1
where the time goes:
time: 169 us; the launch traced here: 168 us
  other arithmetic  50.1 us (30%)
  waiting for transfers between devices  39.4 us (23%)
  matrix products  31.5 us (19%)
  local copies, waits for them, and re-layouts  13.8 us (8%)
  between operations  13.6 us (8%)
  starting transfers between devices  10.1 us (6%)
  blocking collectives  9.97 us (6%)
    another operation x3, other arithmetic  36.6 us
    reduce_scatter x1, waiting for transfers between devices, local(): lax.psum_scatter(jnp.einsum('tak,aksc->stc', band_table_part, stacked, pr...  25.6 us
    all_to_all x1, waiting for transfers between devices, local(): lax.all_to_all(whitened, 'win', split_axis=2, concat_axis=0, tiled=True)  13.3 us
    all_gather x1, blocking collectives, local(): spectra = lax.all_gather(chosen, 'chan', axis=3, tiled=True)  9.97 us
    neg x1, other arithmetic, fourier_table(): return jnp.concatenate([jnp.cos(angles), -jnp.sin(angles)], axis=0)  9.19 us
    dot_general x1, matrix products, local(): jnp.einsum('tak,aksc->stc', band_table_part, stacked, precision=HIGHEST)  9.09 us
    unnamed x11, local copies, waits for them, and re-layouts  7.61 us
    dot_general x1, matrix products, local(): jnp.einsum('kt,wtc->wkc', forward, whiten_pieces, precision=HIGHEST)  6.57 us
  transfers between devices with their start and end apart: 3, of which 3 were waited for; matrix products, arithmetic and copies ran while one was open for 6% of the time, Pallas kernels for 0%

commit v1 on v0

--- a/solution.py
+++ b/solution.py
@@ -82,7 +82,10 @@
     )
     selector = (owned_local[:, None] == channel_ids[None, :]).astype(jnp.float32)
     chosen = jnp.einsum("sc,wafc->wafs", selector, band_data, precision=HIGHEST)
-    spectra = lax.all_gather(chosen, "chan", axis=3, tiled=True)
+    size = lax.axis_size("chan")
+    parts = jnp.stack([chosen for _ in range(size)])
+    parts = lax.all_to_all(parts, "chan", split_axis=0, concat_axis=0)
+    spectra = jnp.concatenate(parts, axis=3)
     source_real = spectra[:, 0]
     source_imag = spectra[:, 1]
     white_real = band_data[:, 0]

time: 169 us -> 171 us (1.012)
  blocking collectives: 9.97 us -> 0 us
  waiting for transfers between devices: 39.4 us -> 46.9 us
  starting transfers between devices: 10.1 us -> 14.1 us
    all_gather x1 -> x0, blocking collectives: 9.97 us -> none  [local(): spectra = lax.all_gather(chosen, 'chan', axis=3, tiled=True)]
    all_to_all x0 -> x1, waiting for transfers between devices: none -> 7.18 us  [local(): parts = lax.all_to_all(parts, 'chan', split_axis=0, concat_axis=0)]
    all_to_all x0 -> x1, starting transfers between devices: none -> 3.81 us  [local(): parts = lax.all_to_all(parts, 'chan', split_axis=0, concat_axis=0)]
  transfers between devices with their start and end apart: 3 -> 4, of which waited for: 3 -> 4; matrix products, arithmetic and copies ran while one was open for 6% -> 7% of each run, Pallas kernels for 0% -> 0%
where the time goes in v1:
time: 171 us
  other arithmetic  50.1 us (29%)
  waiting for transfers between devices  46.9 us (27%)
  matrix products  32.8 us (19%)
  starting transfers between devices  14.1 us (8%)
  between operations  13.6 us (8%)
  local copies, waits for them, and re-layouts  13 us (8%)
    another operation x3, other arithmetic  36.6 us
    reduce_scatter x1, waiting for transfers between devices, local(): lax.psum_scatter(jnp.einsum('tak,aksc->stc', band_table_part, stacked, pr...  24.7 us
    all_to_all x1, waiting for transfers between devices, local(): lax.all_to_all(whitened, 'win', split_axis=2, concat_axis=0, tiled=True)  14.5 us
    neg x1, other arithmetic, fourier_table(): return jnp.concatenate([jnp.cos(angles), -jnp.sin(angles)], axis=0)  9.17 us
    dot_general x1, matrix products, local(): jnp.einsum('tak,aksc->stc', band_table_part, stacked, precision=HIGHEST)  9.1 us
    unnamed x11, local copies, waits for them, and re-layouts  7.53 us
    all_to_all x1, waiting for transfers between devices, local(): parts = lax.all_to_all(parts, 'chan', split_axis=0, concat_axis=0)  7.18 us
    dot_general x1, matrix products, local(): jnp.einsum('kt,wtc->wkc', forward, whiten_pieces, precision=HIGHEST)  6.56 us
  transfers between devices with their start and end apart: 4, of which 4 were waited for; matrix products, arithmetic and copies ran while one was open for 7% of the time, Pallas kernels for 0%

profile of v1, /device:TPU:0, one launch (start us, length us, event | category | flops | bytes accessed | tf_op | source)
XLA Modules:
  0.0 170.6 jit_solution(17390002214347085035)
XLA Ops:
  6.5 2.0 %copy.54 = f32[4,128,256]{1,0,2:T(4,128)} copy(f32[4,128,256]{2,1,0:T(8,128)} %param.2) | data formatting | bytes 1048576 | tf_op args[0]
  8.6 5.2 %all-to-all-start = ((f32[4,128,256]{1,0,2:T(4,128)}), f32[4,128,256]{1,0,2:T(4,128)S(1)}, u32[]{:S(2)}, u32[]{:S(2)}) async-start(f32[4,128,256]{1,0,2:T(4,128)} %copy.54), calls=%async_computation | async-start | bytes 1048576 | tf_op jit(solution)/shard_map/all_to_all | solution.py:58
  13.8 9.2 %sine_negate_fusion = (f32[512,1024]{1,0:T(8,128)}, f32[512,1024]{1,0:T(8,128)}) fusion(), kind=kLoop, calls=%fused_computation.15 | loop fusion | flops 7864320 | bytes 4194304 | tf_op jit(solution)/shard_map/neg | solution.py:17
  22.9 0.5 all-to-all-done
  23.6 0.2 abs_bitcast_fusion
  23.9 0.1 reshape.202
  24.0 36.3 %reduce-window.6 = f32[4,32,9,128]{3,2,1,0:T(8,128)S(1)} reduce-window(f32[4,32,9,128]{3,2,1,0:T(8,128)S(1)} %reshape.202, f32[]{:T(128)} %constant.22.clone.1), window={size=1x1x1x128 pad=0_0x0_0x0_0x127_0}, to_apply=%region_0.1 | reduce-window | flops 18726912 | bytes 1179652 | tf_op jit(solution)/shard_map/reduce-window
  60.2 0.3 slice.45
  60.6 0.4 copy.57
  61.0 0.1 copy.58
  61.1 0.3 broadcast_add_fusion
  61.4 0.1 reduce_window_sum.16
  61.5 6.6 %fusion.14 = f32[4,1024,32]{1,2,0:T(8,128)S(1)} fusion(f32[512,1024]{1,0:T(8,128)} %get-tuple-element.13, f32[512,1024]{1,0:T(8,128)} %get-tuple-element.14, f32[4,1056,32]{1,2,0:T(8,128)S(1)} %bitcast.91, f32[4,1152,32]{1,2,0:T(8,128)S(1)} %bitcast.90, f32[4,8,4,8,128]{4,3,2,1,0:T(8,128)S(1)} %bitcast.87), kind=kOutput, calls=%fused_computation.20 | convolution fusion | flops 1612185600 | bytes 6356992 | tf_op jit(solution)/shard_map/kt,wtc->wkc/dot_general | solution.py:62
  68.1 0.7 divide_bitcast_fusion.1
  68.8 1.1 copy.59
  69.9 0.0 copy-start.2
  69.9 2.1 %reshape.211 = f32[4,1,32768]{2,1,0:T(1,128)} reshape(f32[512,2,4,32]{3,2,1,0:T(4,128)S(1)} %bitcast.82) | data formatting | bytes 1048576
  72.0 4.9 %all-to-all-start.1 = ((f32[4,1,32768]{2,1,0:T(1,128)}), f32[4,1,32768]{2,1,0:T(1,128)S(1)}, u32[]{:S(2)}, u32[]{:S(2)}) async-start(f32[4,1,32768]{2,1,0:T(1,128)} %reshape.211), calls=%async_computation.1 | async-start | bytes 1048576 | tf_op jit(solution)/shard_map/all_to_all | solution.py:72
  76.9 0.0 copy-done.2
  76.9 0.1 dynamic-slice_subtract_fusion
  77.0 14.5 %all-to-all-done.1 = f32[4,1,32768]{2,1,0:T(1,128)S(1)} async-done(((f32[4,1,32768]{2,1,0:T(1,128)}), f32[4,1,32768]{2,1,0:T(1,128)S(1)}, u32[]{:S(2)}, u32[]{:S(2)}) %all-to-all-start.1) | async-done | bytes 524320 | tf_op jit(solution)/shard_map/all_to_all | solution.py:72
  91.5 0.5 broadcast.247
  92.0 2.1 %reduce = f32[4,32768]{1,0:T(4,128)S(1)} reduce(f32[4,1,32768]{2,1,0:T(1,128)S(1)} %all-to-all-done.1, f32[]{:T(128)} %broadcast.247), dimensions={1}, to_apply=%all_to_all.33.reduce_sub_computation | reduce | bytes 1048580 | tf_op jit(solution)/shard_map/all_to_all | solution.py:72
  94.1 1.1 reshape.212
  95.3 0.8 copy.60
  96.1 0.3 fusion.49
  96.4 0.8 stack.32
  97.2 3.8 %all-to-all-start.2 = ((f32[8,16,2,128,4]{3,1,4,2,0:T(8,128)}), f32[8,16,2,128,4]{3,1,4,2,0:T(8,128)S(1)}, u32[]{:S(2)}, u32[]{:S(2)}) async-start(f32[8,16,2,128,4]{3,1,4,2,0:T(8,128)} %stack.32), calls=%async_computation.2 | async-start | bytes 1048576 | tf_op jit(solution)/shard_map/all_to_all | solution.py:87
  101.0 0.2 reduce-scatter.2.cloned.1.call-start
  101.3 1.3 cosine_multiply_fusion
  102.6 0.5 copy.64
  103.1 0.5 copy.66
  103.6 7.2 %all-to-all-done.2 = f32[8,16,2,128,4]{3,1,4,2,0:T(8,128)S(1)} async-done(((f32[8,16,2,128,4]{3,1,4,2,0:T(8,128)}), f32[8,16,2,128,4]{3,1,4,2,0:T(8,128)S(1)}, u32[]{:S(2)}, u32[]{:S(2)}) %all-to-all-start.2) | async-done | bytes 524320 | tf_op jit(solution)/shard_map/all_to_all | solution.py:87
  110.8 1.4 copy.74
  112.2 0.5 copy.75
  112.8 0.0 copy-start
  112.8 4.9 %fusion.21 = f32[128,32,32]{2,1,0:T(8,128)S(1)} fusion(f32[16,128,32]{2,0,1:T(8,128)S(1)} %copy.64, f32[16,1,128,32]{3,0,2,1:T(8,128)} %copy.74), kind=kOutput, calls=%fused_computation.28 | convolution fusion | flops 25165824 | bytes 1048576 | tf_op jit(solution)/shard_map/wfs,wfc->fsc/dot_general | solution.py:93
  117.7 0.0 copy-done
  117.7 3.6 %fusion.19 = f32[128,32,32]{2,1,0:T(8,128)S(1)} fusion(f32[16,128,32]{2,0,1:T(8,128)S(1)} %copy.66, f32[16,1,128,32]{3,0,2,1:T(8,128)S(1)} %copy-done), kind=kOutput, calls=%fused_computation.26 | convolution fusion | flops 25165824 | bytes 1048576 | tf_op jit(solution)/shard_map/wfs,wfc->fsc/dot_general | solution.py:96
  121.4 3.9 %add_bitcast_fusion = f32[1,128,32,32]{3,2,1,0:T(8,128)S(1)} fusion(f32[128,32,32]{2,1,0:T(8,128)S(1)} %fusion.21, f32[16,128,32]{2,0,1:T(8,128)S(1)} %copy.66, f32[16,1,128,32]{3,0,2,1:T(8,128)S(1)} %copy.75), kind=kOutput, calls=%fused_computation.14 | convolution fusion | flops 25296896 | bytes 1572864 | tf_op jit(solution)/shard_map/wfs,wfc->fsc/dot_general | solution.py:95
  125.3 3.7 %subtract_bitcast_fusion = f32[1,128,32,32]{3,2,1,0:T(8,128)S(1)} fusion(f32[128,32,32]{2,1,0:T(8,128)S(1)} %fusion.19, f32[16,128,32]{2,0,1:T(8,128)S(1)} %copy.64, f32[16,1,128,32]{3,0,2,1:T(8,128)S(1)} %copy.75), kind=kOutput, calls=%fused_computation.13 | convolution fusion | flops 25296896 | bytes 1572864 | tf_op jit(solution)/shard_map/wfs,wfc->fsc/dot_general | solution.py:98
  129.0 0.0 copy-start.1
  129.0 0.6 pad_maximum_fusion
  129.6 0.3 copy-done.1
  129.9 9.1 %fusion.11 = f32[32,256,32]{1,2,0:T(8,128)} fusion(f32[2,128,32,32]{3,2,1,0:T(8,128)S(1)} %pad_maximum_fusion, f32[256,1,128]{2,0,1:T(8,128)S(1)} %copy-done.1, f32[256,1,128]{2,0,1:T(8,128)S(1)} %get-tuple-element.11), kind=kOutput, calls=%fused_computation.19 | convolution fusion | flops 805371904 | bytes 2359296 | tf_op jit(solution)/shard_map/tak,aksc->stc/dot_general | solution.py:106
  139.0 0.0 reduce-scatter.2.cloned.1.call-update
  139.1 24.7 %reduce-scatter.2.cloned.1.call-done = f32[8,256,32]{1,2,0:T(8,128)} async-done(((f32[32,256,32]{1,2,0:T(8,128)}), f32[8,256,32]{1,2,0:T(8,128)}) %reduce-scatter.2.cloned.1.call-update) | async-done | bytes 262160 | tf_op jit(solution)/shard_map/reduce_scatter | solution.py:105
  (13 shorter events, 0.3 us)
Async XLA Ops:
  8.6 14.9 %all-to-all-start = ((f32[4,128,256]{1,0,2:T(4,128)}), f32[4,128,256]{1,0,2:T(4,128)S(1)}, u32[]{:S(2)}, u32[]{:S(2)}) async-start(f32[4,128,256]{1,0,2:T(4,128)} %copy.54), calls=%async_computation | async-start | bytes 1048576 | tf_op jit(solution)/shard_map/all_to_all | solution.py:58
  69.9 6.9 %copy-start.2 = (s32[32]{0:T(128)S(1)}, s32[32]{0:T(128)}, u32[]{:S(2)}) copy-start(s32[32]{0:T(128)} %param.3) | copy-start | bytes 388
  72.0 19.5 %all-to-all-start.1 = ((f32[4,1,32768]{2,1,0:T(1,128)}), f32[4,1,32768]{2,1,0:T(1,128)S(1)}, u32[]{:S(2)}, u32[]{:S(2)}) async-start(f32[4,1,32768]{2,1,0:T(1,128)} %reshape.211), calls=%async_computation.1 | async-start | bytes 1048576 | tf_op jit(solution)/shard_map/all_to_all | solution.py:72
  97.2 13.5 %all-to-all-start.2 = ((f32[8,16,2,128,4]{3,1,4,2,0:T(8,128)}), f32[8,16,2,128,4]{3,1,4,2,0:T(8,128)S(1)}, u32[]{:S(2)}, u32[]{:S(2)}) async-start(f32[8,16,2,128,4]{3,1,4,2,0:T(8,128)} %stack.32), calls=%async_computation.2 | async-start | bytes 1048576 | tf_op jit(solution)/shard_map/all_to_all | solution.py:87
  101.0 62.7 %reduce-scatter.2.cloned.1.call-start = ((), (), s32[]{:S(2)}) async-start(), calls=%async_computation.4 | async-start | bytes 1310720 | tf_op jit(solution)/shard_map/reduce_scatter | solution.py:105
  112.8 4.9 %copy-start = (f32[16,1,128,32]{3,0,2,1:T(8,128)S(1)}, f32[16,1,128,32]{3,0,2,1:T(8,128)}, u32[]{:S(2)}) copy-start(f32[16,1,128,32]{3,0,2,1:T(8,128)} %copy.74) | copy-start | bytes 786436
  129.0 0.9 copy-start.1
Sparse Core Ops, SparseCore 0:
  139.2 24.5 reduce-scatter.1
